TPU v7x, 256 devices: a whole 4x4x8 slice. The times are simulated.
256 devices in a mesh: freq: 16 (over z, core), bl: 16 (over y, x).
Axes of the slice: x: 4, y: 4, z: 8, core: 2. Of those that a mesh axis runs over, the one named last changes fastest.
Arguments:
- visibilities: float32 [2, 64, 4, 131072], P(None, 'freq', None, 'bl')
- sky_model: bfloat16 [2, 64, 8, 4, 131072], P(None, 'freq', None, None, 'bl')
- flag_mask: int32 [4, 131072], P(None, 'bl'), may hold values from 0 to 1
- first_station: int32 [131072], P('bl'), may hold values from 0 to 511
- second_station: int32 [131072], P('bl'), may hold values from 0 to 511, as said below
- gain_start: float32 [2, 64, 8, 512], P(None, 'freq')
- dual_start: float32 [2, 64, 8, 512], P(None, 'freq'), may hold values from -1.8 to 1.8
- consensus_start: float32 [3, 2, 8, 512], replicated, may hold values from -27.495455 to 27.495455
- penalty: float32 [8], replicated, may hold values from 0.3 to 3
Outputs:
- gain_final: float32 [2, 64, 8, 512], P(None, 'freq')
- dual_final: float32 [2, 64, 8, 512], P(None, 'freq')
- consensus_final: float32 [3, 2, 8, 512], replicated
Inputs may be any that keep to these rules, and one draw needn't show every extreme that they name: `second_station`: differs from first_station on every baseline.
All inputs are finite; a program needn't handle non-finite values.
Results may differ from a plain program's by a relative error of at most 0.0003.
Values sent between devices are 32-bit elements; how exact they have to be, the bound alone decides.
No kernel may reach another device: no remote copies, remote signals or barrier semaphores. Data moves between devices by JAX's collectives and lax.ppermute only.
A program may use at most 64 MiB of HBM per device.

v0:
```python
import math
import jax
import jax.numpy as jnp
from jax import lax
from jax.sharding import PartitionSpec as P

NPOLY = 3
NIT = 3
precise = lax.Precision.HIGHEST


def poly_basis(channel_count, degree):
    positions = jnp.arange(channel_count).astype(jnp.float32)
    spread = (2.0 * positions + 1.0) / channel_count - 1.0
    columns = []
    for exponent in range(degree):
        column = spread**exponent
        for earlier in columns:
            column = column - jnp.sum(column * earlier) * earlier
        column = column / jnp.sqrt(jnp.sum(column * column))
        columns.append(column)
    return jnp.stack(columns, axis=1)


def visibility_products(
    sky_real,
    sky_imag,
    vis_real,
    vis_imag,
    weights,
    first_real,
    first_imag,
    second_gain_real,
    second_imag,
):
    apparent_real = sky_real * second_gain_real + sky_imag * second_imag
    apparent_imag = sky_imag * second_gain_real - sky_real * second_imag
    predicted_real = first_real * apparent_real - first_imag * apparent_imag
    predicted_imag = first_real * apparent_imag + first_imag * apparent_real
    leftover_real = weights * (vis_real - jnp.sum(predicted_real, axis=-3))
    leftover_imag = weights * (vis_imag - jnp.sum(predicted_imag, axis=-3))
    target_real = jnp.expand_dims(leftover_real, -3) + weights * predicted_real
    target_imag = jnp.expand_dims(leftover_imag, -3) + weights * predicted_imag
    mirror_real = sky_real * first_real - sky_imag * first_imag
    mirror_imag = sky_real * first_imag + sky_imag * first_real
    first_terms = jnp.stack(
        [
            jnp.sum(apparent_real * target_real + apparent_imag * target_imag, axis=-2),
            jnp.sum(apparent_real * target_imag - apparent_imag * target_real, axis=-2),
            jnp.sum(
                weights * (apparent_real * apparent_real + apparent_imag * apparent_imag), axis=-2
            ),
        ]
    )
    second_terms = jnp.stack(
        [
            jnp.sum(mirror_real * target_real + mirror_imag * target_imag, axis=-2),
            jnp.sum(mirror_imag * target_real - mirror_real * target_imag, axis=-2),
            jnp.sum(weights * (mirror_real * mirror_real + mirror_imag * mirror_imag), axis=-2),
        ]
    )
    return (first_terms, second_terms)


def gain_update(gain_values, summed, target, dual_values, weight):
    denom = summed[2] + weight
    new_real = (summed[0] + weight * target[0] - dual_values[0]) / denom
    new_imag = (summed[1] + weight * target[1] - dual_values[1]) / denom
    return 0.5 * (gain_values + jnp.stack([new_real, new_imag]))


def per_device(
    visibilities,
    sky_model,
    flag_mask,
    first_station,
    second_station,
    gain_start,
    dual_start,
    consensus_start,
    penalty,
):
    local_channels = visibilities.shape[1]
    directions = gain_start.shape[2]
    stations = gain_start.shape[3]
    antenna_pairs = visibilities.shape[3]
    block_length = math.gcd(antenna_pairs, 1024)
    count_of_blocks = antenna_pairs // block_length
    channel_count = local_channels * lax.axis_size("freq")
    basis_rows = poly_basis(channel_count, NPOLY)
    local_rows = lax.dynamic_slice_in_dim(
        basis_rows, lax.axis_index("freq") * local_channels, local_channels, 0
    )
    weight = penalty[:, None]
    target = jnp.einsum("fn,nckp->cfkp", local_rows, consensus_start, precision=precise)
    flag_weight = flag_mask.astype(jnp.float32)
    station_iota = lax.broadcasted_iota(jnp.int32, (stations, block_length), 0)
    contract = (((1,), (1,)), ((), ()))
    rows_total = 3 * local_channels * directions
    gain_now = gain_start
    for iteration in range(NIT):
        gain_table = gain_now.reshape(2 * local_channels * directions, stations)

        def add_block(position, totals):
            block_start = position * block_length
            first_ids = lax.dynamic_slice_in_dim(first_station, block_start, block_length, 0)
            second_station_index = lax.dynamic_slice_in_dim(
                second_station, block_start, block_length, 0
            )
            first_hot = (station_iota == first_ids[None, :]).astype(jnp.float32)
            second_hot = (station_iota == second_station_index[None, :]).astype(jnp.float32)
            first_gain = jnp.dot(
                gain_table, first_hot, precision=precise, preferred_element_type=jnp.float32
            ).reshape(2, local_channels, directions, 1, block_length)
            second_gain = jnp.dot(
                gain_table, second_hot, precision=precise, preferred_element_type=jnp.float32
            ).reshape(2, local_channels, directions, 1, block_length)
            sky_block = lax.dynamic_slice_in_dim(sky_model, block_start, block_length, 4).astype(
                jnp.float32
            )
            vis_block = lax.dynamic_slice_in_dim(visibilities, block_start, block_length, 3)
            mask_block = lax.dynamic_slice_in_dim(flag_weight, block_start, block_length, 1)
            first_terms, second_terms = visibility_products(
                sky_block[0],
                sky_block[1],
                vis_block[0],
                vis_block[1],
                mask_block,
                first_gain[0],
                first_gain[1],
                second_gain[0],
                second_gain[1],
            )
            first_terms = first_terms.reshape(rows_total, block_length)
            second_terms = second_terms.reshape(rows_total, block_length)
            first_sums = lax.dot_general(
                first_terms,
                first_hot,
                contract,
                precision=precise,
                preferred_element_type=jnp.float32,
            )
            second_sums = lax.dot_general(
                second_terms,
                second_hot,
                contract,
                precision=precise,
                preferred_element_type=jnp.float32,
            )
            return totals + first_sums + second_sums

        totals = lax.fori_loop(
            0, count_of_blocks, add_block, jnp.zeros((rows_total, stations), jnp.float32)
        )
        partial_sums = totals.reshape(3, local_channels, directions, stations)
        summed_all = lax.psum(partial_sums, "bl")
        gain_now = gain_update(gain_now, summed_all, target, dual_start, weight)
    shifted = gain_now + dual_start / weight
    local_part = jnp.einsum("fn,cfkp->nckp", local_rows, shifted, precision=precise)
    consensus_final = lax.psum(local_part, "freq")
    fitted = jnp.einsum("fn,nckp->cfkp", local_rows, consensus_final, precision=precise)
    dual_final = dual_start + weight * (gain_now - fitted)
    return (gain_now, dual_final, consensus_final)


def solution(mesh):
    in_specs = (
        P(None, "freq", None, "bl"),
        P(None, "freq", None, None, "bl"),
        P(None, "bl"),
        P("bl"),
        P("bl"),
        P(None, "freq", None, None),
        P(None, "freq", None, None),
        P(),
        P(),
    )
    out_specs = (P(None, "freq", None, None), P(None, "freq", None, None), P())
    return jax.shard_map(
        per_device, mesh=mesh, in_specs=in_specs, out_specs=out_specs, check_vma=False
    )
```

profile of v0, /device:TPU:1, one launch (start us, length us, event | category | flops | bytes accessed | tf_op | source)
XLA Modules:
  0.0 750.2 jit_solution(8116796445936718820)
XLA Ops:
  8.2 106.4 %while.45 = (s32[]{:T(128)}, f32[96,512]{1,0:T(8,128)S(1)}, bf16[2,4,8,4,8192]{4,3,2,1,0:T(4,128)(2,1)}, s32[8192]{0:T(1024)}, f32[64,512]{1,0:T(8,128)}, /*inde...) while((s32[]{:T(128)}, f32[96,512]{1,0:T(8,128)S(1)}, ...), condition=%wide.region_9.10_spmd.clone.clone, body=%wide.region_0.9_spmd.clone.clone.sunk | while | flops 2023342080 | bytes 14123225 | solution.py:152
  16.2 2.8 add_reduce_fusion.9
  29.5 2.8 add_reduce_fusion.9
  42.8 2.8 add_reduce_fusion.9
  56.1 2.8 add_reduce_fusion.9
  69.4 2.8 add_reduce_fusion.9
  82.7 2.8 add_reduce_fusion.9
  96.0 2.8 add_reduce_fusion.9
  109.3 2.8 add_reduce_fusion.9
  123.5 88.3 %all-reduce.5.cloned.1.call-done = f32[3,4,8,512]{3,1,2,0:T(4,128)} async-done(((f32[3,4,8,512]{3,1,2,0:T(4,128)}), f32[3,4,8,512]{3,1,2,0:T(4,128)}) %all-reduce.5.cloned.1.call-update) | async-done | bytes 196624 | tf_op jit(solution)/shard_map/psum | solution.py:156
  214.6 106.4 %while.46 = (s32[]{:T(128)}, f32[96,512]{1,0:T(8,128)}, bf16[2,4,8,4,8192]{4,3,2,1,0:T(4,128)(2,1)}, s32[8192]{0:T(1024)S(1)}, f32[64,512]{1,0:T(8,128)}, /*inde...) while((s32[]{:T(128)}, f32[96,512]{1,0:T(8,128)}, ...), condition=%wide.region_25.26_spmd.clone.clone, body=%wide.region_16.25_spmd.clone.clone.sunk | while | flops 2023342080 | bytes 15696145 | solution.py:152
  221.9 2.8 add_reduce_fusion.10
  235.2 2.8 add_reduce_fusion.10
  248.5 2.8 add_reduce_fusion.10
  288.3 2.8 add_reduce_fusion.10
  314.9 2.8 add_reduce_fusion.10
  323.0 93.6 %all-reduce.7.cloned.1.call-done = f32[3,4,8,512]{3,1,2,0:T(4,128)} async-done(((f32[3,4,8,512]{3,1,2,0:T(4,128)}), f32[3,4,8,512]{3,1,2,0:T(4,128)}) %all-reduce.7.cloned.1.call-update) | async-done | bytes 196624 | tf_op jit(solution)/shard_map/psum | solution.py:156
  418.5 111.6 %while.47 = (s32[]{:T(128)}, f32[96,512]{1,0:T(8,128)}, bf16[2,4,8,4,8192]{4,3,2,1,0:T(4,128)(2,1)}, s32[8192]{0:T(1024)S(1)}, f32[64,512]{1,0:T(8,128)}, /*inde...) while((s32[]{:T(128)}, f32[96,512]{1,0:T(8,128)}, ...), condition=%wide.region_36.37_spmd.clone.clone, body=%wide.region_27.36_spmd.clone.clone.sunk | while | flops 2023342080 | bytes 15761793 | solution.py:152
  426.4 2.8 add_reduce_fusion.11
  496.1 2.8 add_reduce_fusion.11
  510.1 2.8 add_reduce_fusion.11
  524.0 2.8 add_reduce_fusion.11
  531.9 93.8 %all-reduce.9.cloned.1.call-done = f32[3,4,8,512]{3,1,2,0:T(4,128)} async-done(((f32[3,4,8,512]{3,1,2,0:T(4,128)}), f32[3,4,8,512]{3,1,2,0:T(4,128)}) %all-reduce.9.cloned.1.call-update) | async-done | bytes 196624 | tf_op jit(solution)/shard_map/psum | solution.py:156
  629.4 110.6 %all-reduce.11.cloned.1.call-done = f32[3,2,8,512]{3,0,2,1:T(4,128)} async-done(((f32[3,2,8,512]{3,0,2,1:T(4,128)}), f32[3,2,8,512]{3,0,2,1:T(4,128)}) %all-reduce.11.cloned.1.call-update) | async-done | bytes 98320 | tf_op jit(solution)/shard_map/psum | solution.py:160
  (501 shorter events, 295.9 us)
Async XLA Ops:
  7.2 115.8 %copy-start = (f32[3,2,8,512]{3,2,1,0:T(8,128)S(1)}, f32[3,2,8,512]{3,2,1,0:T(8,128)}, u32[]{:S(2)}) copy-start(f32[3,2,8,512]{3,2,1,0:T(8,128)} %param.22) | copy-start | bytes 294916
  7.2 204.6 %all-reduce.5.cloned.1.call-start = ((), (), s32[]{:S(2)}) async-start(), calls=%async_computation | async-start | bytes 393216 | tf_op jit(solution)/shard_map/psum | solution.py:156
  8.2 114.6 %copy-start.2 = (f32[2,4,8,512]{3,2,1,0:T(8,128)S(1)}, f32[2,4,8,512]{3,2,1,0:T(8,128)}, u32[]{:S(2)}) copy-start(f32[2,4,8,512]{3,2,1,0:T(8,128)} %param.21) | copy-start | bytes 393220
  8.2 203.7 %copy-start.14 = (f32[8]{0:T(128)S(1)}, f32[8]{0:T(128)}, u32[]{:S(2)}) copy-start(f32[8]{0:T(128)} %param.23) | copy-start | bytes 100
  114.6 100.0 %copy-start.7 = (s32[8192]{0:T(1024)S(1)}, s32[8192]{0:T(1024)}, u32[]{:S(2)}) copy-start(s32[8192]{0:T(1024)} %get-tuple-element.1150) | copy-start | bytes 98308
  115.5 301.2 %all-reduce.7.cloned.1.call-start = ((), (), s32[]{:S(2)}) async-start(), calls=%async_computation.1 | async-start | bytes 393216 | tf_op jit(solution)/shard_map/psum | solution.py:156
  214.6 203.1 %copy-start.1 = (f32[64,512]{1,0:T(8,128)S(1)}, f32[64,512]{1,0:T(8,128)}, u32[]{:S(2)}) copy-start(f32[64,512]{1,0:T(8,128)} %get-tuple-element.1135) | copy-start | bytes 393220
  221.9 4.1 copy-start.3
  235.2 4.1 copy-start.3
  261.7 4.1 copy-start.3
  288.3 4.1 copy-start.3
  314.9 4.1 copy-start.3
  322.7 303.0 %all-reduce.9.cloned.1.call-start = ((), (), s32[]{:S(2)}) async-start(), calls=%async_computation.2 | async-start | bytes 393216 | tf_op jit(solution)/shard_map/psum | solution.py:156
  426.4 4.2 copy-start.9
  440.3 4.2 copy-start.9
  454.3 4.2 copy-start.9
  468.2 4.2 copy-start.9
  482.2 4.2 copy-start.9
  496.1 4.2 copy-start.9
  510.0 4.2 copy-start.9
  524.0 4.2 copy-start.9
  530.1 210.0 %copy-start.13 = (f32[64,3]{0,1:T(4,128)S(1)}, f32[64,3]{0,1:T(4,128)}, u32[]{:S(2)}) copy-start(f32[64,3]{0,1:T(4,128)} %copy-done.12) | copy-start | bytes 2308
  530.1 210.0 %copy-start.15 = (f32[8]{0:T(128)S(1)}, f32[8]{0:T(128)}, u32[]{:S(2)}) copy-start(f32[8]{0:T(128)} %param.23) | copy-start | bytes 100
  531.8 208.2 %all-reduce.11.cloned.1.call-start = ((), (), s32[]{:S(2)}) async-start(), calls=%async_computation.3 | async-start | bytes 262144 | tf_op jit(solution)/shard_map/psum | solution.py:160
  (52 other events, 77.0 us)
Sparse Core Ops, SparseCore 0:
  115.6 96.2 all-reduce.4
  322.8 93.7 all-reduce.6
  532.0 93.7 all-reduce.8
  628.9 111.1 all-reduce.10
where the time goes:
time: 755 us; the launch traced here: 750 us
  waiting for transfers between devices  386 us (51%)
  other arithmetic  148 us (20%)
  matrix products  147 us (19%)
  local copies, waits for them, and re-layouts  47.9 us (6%)
  between operations  16.6 us (2%)
    psum x3, waiting for transfers between devices, per_device(): summed_all = lax.psum(partial_sums, 'bl')  276 us
    psum x1, waiting for transfers between devices, per_device(): consensus_final = lax.psum(local_part, 'freq')  111 us
    reduce_sum x24, other arithmetic, visibility_products(): jnp.sum(mirror_real * target_real + mirror_imag * target_imag, axis=-2)  67.9 us
    dot_general x24, matrix products, add_block(): jnp.dot(gain_table, second_hot, precision=precise, preferred_element_type...  42.6 us
    dot_general x24, matrix products, add_block(): jnp.dot(gain_table, first_hot, precision=precise, preferred_element_type=...  42.6 us
    dot_general x24, matrix products, add_block(): lax.dot_general(first_terms, first_hot, contract, precision=precise, pref...  29.2 us
    dot_general x24, matrix products, add_block(): lax.dot_general(second_terms, second_hot, contract, precision=precise, pr...  28.8 us
    convert_element_type x24, other arithmetic, add_block(): lax.dynamic_slice_in_dim(sky_model, block_start, block_length, 4)  28.2 us
  transfers between devices with their start and end apart: 4, of which 4 were waited for; matrix products, arithmetic and copies ran while one was open for 1% of the time, Pallas kernels for 0%

commit v1 on v0

--- a/solution.py
+++ b/solution.py
@@ -1,3 +1,4 @@
+import functools
 import math
 import jax
 import jax.numpy as jnp
@@ -7,6 +8,14 @@
 NPOLY = 3
 NIT = 3
 precise = lax.Precision.HIGHEST
+
+
+def _manage_task(packet, along_axis):
+    t1 = jnp.sum(lax.all_gather(packet, axis_name=along_axis), 0)
+    return t1
+
+
+lead_ways = functools.partial(_manage_task, along_axis="freq")
 
 
 def poly_basis(channel_count, degree):
@@ -157,7 +166,7 @@
         gain_now = gain_update(gain_now, summed_all, target, dual_start, weight)
     shifted = gain_now + dual_start / weight
     local_part = jnp.einsum("fn,cfkp->nckp", local_rows, shifted, precision=precise)
-    consensus_final = lax.psum(local_part, "freq")
+    consensus_final = lead_ways(local_part)
     fitted = jnp.einsum("fn,nckp->cfkp", local_rows, consensus_final, precision=precise)
     dual_final = dual_start + weight * (gain_now - fitted)
     return (gain_now, dual_final, consensus_final)

time: 755 us -> 683 us (0.905)
  waiting for transfers between devices: 386 us -> 316 us
    psum x1 -> x0, waiting for transfers between devices: 111 us -> none  [per_device(): consensus_final = lax.psum(local_part, 'freq')]
    all_gather x0 -> x1, waiting for transfers between devices: none -> 40.1 us  [_manage_task(): t1 = jnp.sum(lax.all_gather(packet, axis_name=along_axis), 0)]
where the time goes in v1:
time: 683 us; the launch traced here: 679 us
  waiting for transfers between devices  316 us (46%)
  other arithmetic  150 us (22%)
  matrix products  145 us (21%)
  local copies, waits for them, and re-layouts  46.9 us (7%)
  between operations  16.6 us (2%)
    psum x3, waiting for transfers between devices, per_device(): summed_all = lax.psum(partial_sums, 'bl')  276 us
    reduce_sum x24, other arithmetic, visibility_products(): jnp.sum(mirror_real * target_real + mirror_imag * target_imag, axis=-2)  67.6 us
    dot_general x24, matrix products, add_block(): jnp.dot(gain_table, first_hot, precision=precise, preferred_element_type=...  42.6 us
    dot_general x24, matrix products, add_block(): jnp.dot(gain_table, second_hot, precision=precise, preferred_element_type...  42.6 us
    all_gather x1, waiting for transfers between devices, _manage_task(): t1 = jnp.sum(lax.all_gather(packet, axis_name=along_axis), 0)  40.1 us
    dot_general x24, matrix products, add_block(): lax.dot_general(first_terms, first_hot, contract, precision=precise, pref...  29.2 us
    dot_general x24, matrix products, add_block(): lax.dot_general(second_terms, second_hot, contract, precision=precise, pr...  28.8 us
    convert_element_type x24, other arithmetic, add_block(): lax.dynamic_slice_in_dim(sky_model, block_start, block_length, 4)  28.2 us
  transfers between devices with their start and end apart: 4, of which 4 were waited for; matrix products, arithmetic and copies ran while one was open for 1% of the time, Pallas kernels for 0%

profile of v1, /device:TPU:1, one launch (start us, length us, event | category | flops | bytes accessed | tf_op | source)
XLA Modules:
  0.0 678.6 jit_solution(7625958357424246029)
XLA Ops:
  8.2 106.3 %while.45 = (s32[]{:T(128)}, f32[96,512]{1,0:T(8,128)S(1)}, bf16[2,4,8,4,8192]{4,3,2,1,0:T(4,128)(2,1)}, s32[8192]{0:T(1024)}, f32[64,512]{1,0:T(8,128)}, /*inde...) while((s32[]{:T(128)}, f32[96,512]{1,0:T(8,128)S(1)}, ...), condition=%wide.region_9.10_spmd.clone.clone, body=%wide.region_0.9_spmd.clone.clone.sunk | while | flops 2023342080 | bytes 14123225 | solution.py:161
  16.2 2.8 add_reduce_fusion.9
  123.3 88.3 %all-reduce.4.cloned.1.call-done = f32[3,4,8,512]{3,1,2,0:T(4,128)} async-done(((f32[3,4,8,512]{3,1,2,0:T(4,128)}), f32[3,4,8,512]{3,1,2,0:T(4,128)}) %all-reduce.4.cloned.1.call-update) | async-done | bytes 196624 | tf_op jit(solution)/shard_map/psum | solution.py:165
  214.4 106.4 %while.46 = (s32[]{:T(128)}, f32[96,512]{1,0:T(8,128)}, bf16[2,4,8,4,8192]{4,3,2,1,0:T(4,128)(2,1)}, s32[8192]{0:T(1024)S(1)}, f32[64,512]{1,0:T(8,128)}, /*inde...) while((s32[]{:T(128)}, f32[96,512]{1,0:T(8,128)}, ...), condition=%wide.region_25.26_spmd.clone.clone, body=%wide.region_16.25_spmd.clone.clone.sunk | while | flops 2023342080 | bytes 15696145 | solution.py:161
  221.7 2.8 add_reduce_fusion.10
  235.0 2.8 add_reduce_fusion.10
  248.3 2.8 add_reduce_fusion.10
  261.6 2.8 add_reduce_fusion.10
  274.9 2.8 add_reduce_fusion.10
  288.2 2.8 add_reduce_fusion.10
  301.5 2.8 add_reduce_fusion.10
  314.8 2.8 add_reduce_fusion.10
  322.8 93.6 %all-reduce.6.cloned.1.call-done = f32[3,4,8,512]{3,1,2,0:T(4,128)} async-done(((f32[3,4,8,512]{3,1,2,0:T(4,128)}), f32[3,4,8,512]{3,1,2,0:T(4,128)}) %all-reduce.6.cloned.1.call-update) | async-done | bytes 196624 | tf_op jit(solution)/shard_map/psum | solution.py:165
  418.3 111.6 %while.47 = (s32[]{:T(128)}, f32[96,512]{1,0:T(8,128)}, bf16[2,4,8,4,8192]{4,3,2,1,0:T(4,128)(2,1)}, s32[8192]{0:T(1024)S(1)}, f32[64,512]{1,0:T(8,128)}, /*inde...) while((s32[]{:T(128)}, f32[96,512]{1,0:T(8,128)}, ...), condition=%wide.region_36.37_spmd.clone.clone, body=%wide.region_27.36_spmd.clone.clone.sunk | while | flops 2023342080 | bytes 15761793 | solution.py:161
  426.2 2.8 add_reduce_fusion.11
  440.1 2.8 add_reduce_fusion.11
  454.1 2.8 add_reduce_fusion.11
  468.0 2.8 add_reduce_fusion.11
  482.0 2.8 add_reduce_fusion.11
  495.9 2.8 add_reduce_fusion.11
  509.8 2.8 add_reduce_fusion.11
  523.8 2.8 add_reduce_fusion.11
  531.7 93.8 %all-reduce.8.cloned.1.call-done = f32[3,4,8,512]{3,1,2,0:T(4,128)} async-done(((f32[3,4,8,512]{3,1,2,0:T(4,128)}), f32[3,4,8,512]{3,1,2,0:T(4,128)}) %all-reduce.8.cloned.1.call-update) | async-done | bytes 196624 | tf_op jit(solution)/shard_map/psum | solution.py:165
  629.2 40.1 %all-gather.3.cloned.1.call-done = f32[48,2,8,512]{3,2,1,0:T(8,128)} async-done(((f32[3,2,8,512]{3,2,1,0:T(8,128)}), f32[48,2,8,512]{3,2,1,0:T(8,128)}) %all-gather.3.cloned.1.call-update) | async-done | bytes 1572880 | tf_op jit(solution)/shard_map/all_gather | solution.py:14
  (504 shorter events, 294.9 us)
Async XLA Ops:
  7.2 115.6 %copy-start = (f32[3,2,8,512]{3,2,1,0:T(8,128)S(1)}, f32[3,2,8,512]{3,2,1,0:T(8,128)}, u32[]{:S(2)}) copy-start(f32[3,2,8,512]{3,2,1,0:T(8,128)} %param.22) | copy-start | bytes 294916
  7.2 204.5 %all-reduce.4.cloned.1.call-start = ((), (), s32[]{:S(2)}) async-start(), calls=%async_computation | async-start | bytes 393216 | tf_op jit(solution)/shard_map/psum | solution.py:165
  8.2 114.4 %copy-start.3 = (f32[2,4,8,512]{3,2,1,0:T(8,128)S(1)}, f32[2,4,8,512]{3,2,1,0:T(8,128)}, u32[]{:S(2)}) copy-start(f32[2,4,8,512]{3,2,1,0:T(8,128)} %param.21) | copy-start | bytes 393220
  8.2 203.5 %copy-start.15 = (f32[8]{0:T(128)S(1)}, f32[8]{0:T(128)}, u32[]{:S(2)}) copy-start(f32[8]{0:T(128)} %param.23) | copy-start | bytes 100
  114.5 100.0 %copy-start.8 = (s32[8192]{0:T(1024)S(1)}, s32[8192]{0:T(1024)}, u32[]{:S(2)}) copy-start(s32[8192]{0:T(1024)} %get-tuple-element.1150) | copy-start | bytes 98308
  115.3 301.1 %all-reduce.6.cloned.1.call-start = ((), (), s32[]{:S(2)}) async-start(), calls=%async_computation.1 | async-start | bytes 393216 | tf_op jit(solution)/shard_map/psum | solution.py:165
  214.4 203.0 %copy-start.1 = (f32[64,512]{1,0:T(8,128)S(1)}, f32[64,512]{1,0:T(8,128)}, u32[]{:S(2)}) copy-start(f32[64,512]{1,0:T(8,128)} %get-tuple-element.1136) | copy-start | bytes 393220
  221.7 4.1 copy-start.4
  235.0 4.1 copy-start.4
  261.6 4.1 copy-start.4
  288.2 4.1 copy-start.4
  314.8 4.1 copy-start.4
  322.6 302.9 %all-reduce.8.cloned.1.call-start = ((), (), s32[]{:S(2)}) async-start(), calls=%async_computation.2 | async-start | bytes 393216 | tf_op jit(solution)/shard_map/psum | solution.py:165
  426.2 4.2 copy-start.10
  440.1 4.2 copy-start.10
  454.1 4.2 copy-start.10
  468.0 4.2 copy-start.10
  481.9 4.2 copy-start.10
  495.9 4.2 copy-start.10
  509.8 4.2 copy-start.10
  523.8 4.2 copy-start.10
  531.6 137.7 %all-gather.3.cloned.1.call-start = ((), (), s32[]{:S(2)}) async-start(), calls=%async_computation.3 | async-start | bytes 1671168 | tf_op jit(solution)/shard_map/all_gather | solution.py:14
  626.5 44.4 %copy-start.14 = (f32[64,3]{0,1:T(4,128)S(1)}, f32[64,3]{0,1:T(4,128)}, u32[]{:S(2)}) copy-start(f32[64,3]{0,1:T(4,128)} %copy-done.13) | copy-start | bytes 2308
  626.5 44.4 %copy-start.16 = (f32[8]{0:T(128)S(1)}, f32[8]{0:T(128)}, u32[]{:S(2)}) copy-start(f32[8]{0:T(128)} %param.23) | copy-start | bytes 100
  (53 other events, 78.2 us)
Sparse Core Ops, SparseCore 0:
  115.4 96.2 all-reduce.3
  322.7 93.6 all-reduce.5
  531.7 93.6 all-reduce.7
  628.6 40.6 all-gather.2
